TPU v7x, 32 devices: a whole 2x2x4 slice. The times are simulated.
32 devices in a mesh: grp: 2 (over y), freq: 4 (over z), panel: 4 (over x, core).
Axes of the slice: x: 2, y: 2, z: 4, core: 2. Of those that a mesh axis runs over, the one named last changes fastest.
Arguments:
- traces: float32 [1024, 3072], P('freq', ('grp', 'panel')), parts along dimension 1, may hold values from -6 to 6
- centroids: float32 [3, 3072], P(None, ('grp', 'panel')), parts along dimension 1, may hold values from -1 to 1
- near_list: int32 [8, 8, 2], P(('grp', 'panel')), parts along dimension 0, may hold values from 0 to 4, as said below
- pair_count: int32 [8], P(('grp', 'panel')), parts along dimension 0, may hold values from 5 to 8, as said below
Outputs:
- field: float32 [1024, 3072], P('freq', ('grp', 'panel')), parts along dimension 1
There are 2 independent parts, one for each index of `grp`. A program takes and returns all parts, laid end to end along the dimension named above; each array names one. Nothing has to cross between parts.
Inputs may be any that keep to these rules, and one draw needn't show every extreme that they name: `near_list`: each row holds a row block below 3 and an extended column block up to 4; in every shard, pair n < 3 is (n, n + 1), pair 3 is (0, 0) and pair 4 is (2, 4); pairs may repeat; entries past the count are valid but unused. `pair_count`: some shard holds 8 pairs in every draw.
All inputs are finite; a program needn't handle non-finite values.
Results may differ from a plain program's by a relative error of at most 0.0003.
Values sent between devices are 32-bit elements; how exact they have to be, the bound alone decides.
A program may use at most 64 MiB of HBM per device.

v0:
```python
import math

import jax
import jax.numpy as jnp
from jax import lax
from jax.sharding import PartitionSpec as P

NT = 1024
BLK = 128


damping = 0.999
time_step = 0.5
core_square = 0.01
highest = lax.Precision.HIGHEST


def extended(x, sides, width):
    for axis, dim in sides:
        size, length = (lax.axis_size(axis), x.shape[dim])
        up = [(i, (i + 1) % size) for i in range(size)]
        down = [(j, i) for i, j in up]
        last = lax.slice_in_dim(x, length - width, length, axis=dim)
        initial = lax.slice_in_dim(x, 0, width, axis=dim)
        before = lax.ppermute(last, axis, up)
        after = lax.ppermute(initial, axis, down)
        x = jnp.concatenate([before, x, after], axis=dim)
    return x


def forward_tables(times, freqs):
    product = freqs[:, None] * times[None, :] % NT
    angle = 2.0 * math.pi / NT * product.astype(jnp.float32)
    decay = jnp.exp(times.astype(jnp.float32) * math.log(damping))
    return (jnp.cos(angle) * decay[None, :], -jnp.sin(angle) * decay[None, :])


def inverse_tables(times, freqs):
    product = times[:, None] * freqs[None, :] % NT
    angle = 2.0 * math.pi / NT * product.astype(jnp.float32)
    growth = jnp.exp(-times.astype(jnp.float32) * math.log(damping)) / NT
    weight = jnp.where(freqs == 0, 1.0, 2.0).astype(jnp.float32)
    scale = growth[:, None] * weight[None, :]
    return (jnp.cos(angle) * scale, jnp.sin(angle) * scale)


def laplace(freqs):
    angle = 2.0 * math.pi / NT * freqs.astype(jnp.float32)
    return ((1.0 - damping * jnp.cos(angle)) / time_step, damping * jnp.sin(angle) / time_step)


def block_kernel(rows_xyz, cols_xyz, lap_re, lap_im):
    diff = rows_xyz[:, :, None] - cols_xyz[:, None, :]
    dist = jnp.sqrt(jnp.sum(diff * diff, axis=0) + core_square)
    decay = jnp.exp(-lap_re[:, None, None] * dist[None]) / (4.0 * math.pi * dist[None])
    phase = lap_im[:, None, None] * dist[None]
    return (decay * jnp.cos(phase), -decay * jnp.sin(phase))


def apply_pairs(ext_re, ext_im, ext_xyz, shard_list, count, lap_re, lap_im):
    kcount = ext_re.shape[0]
    own = ext_re.shape[1] - 2 * BLK

    def add_pair(slot, acc):
        acc_re, acc_im = acc
        row = shard_list[slot, 0]
        col = shard_list[slot, 1]
        rows_xyz = lax.dynamic_slice_in_dim(ext_xyz, (row + 1) * BLK, BLK, 1)
        cols_xyz = lax.dynamic_slice_in_dim(ext_xyz, col * BLK, BLK, 1)
        g_re = lax.dynamic_slice_in_dim(ext_re, col * BLK, BLK, 1)
        g_im = lax.dynamic_slice_in_dim(ext_im, col * BLK, BLK, 1)
        k_re, k_im = block_kernel(rows_xyz, cols_xyz, lap_re, lap_im)
        new_re = jnp.einsum("kij,kj->ki", k_re, g_re, precision=highest) - jnp.einsum(
            "kij,kj->ki", k_im, g_im, precision=highest
        )
        new_im = jnp.einsum("kij,kj->ki", k_re, g_im, precision=highest) + jnp.einsum(
            "kij,kj->ki", k_im, g_re, precision=highest
        )
        start = row * BLK
        acc_re = lax.dynamic_update_slice_in_dim(
            acc_re, lax.dynamic_slice_in_dim(acc_re, start, BLK, 1) + new_re, start, 1
        )
        acc_im = lax.dynamic_update_slice_in_dim(
            acc_im, lax.dynamic_slice_in_dim(acc_im, start, BLK, 1) + new_im, start, 1
        )
        return (acc_re, acc_im)

    zeros = jnp.zeros((kcount, own), jnp.float32)
    return lax.fori_loop(jnp.int32(0), count, add_pair, (zeros, zeros))


def per_device(traces, centroids, near_list, pair_count):
    groups = lax.axis_size("freq")
    slab_times = traces.shape[0]
    width = traces.shape[1]
    total_times = slab_times * groups
    half = total_times // 2
    slab_freqs = half // groups
    position = lax.axis_index("freq")
    own_times = position * slab_times + jnp.arange(slab_times, dtype=jnp.int32)
    own_freqs = position * slab_freqs + jnp.arange(slab_freqs, dtype=jnp.int32)
    freqs = jnp.arange(slab_freqs * lax.axis_size("freq"), dtype=jnp.int32)
    fcos, fsin = forward_tables(own_times, freqs)
    part_re = jnp.dot(fcos, traces, precision=highest)
    part_im = jnp.dot(fsin, traces, precision=highest)
    spectrum = lax.psum_scatter(
        jnp.concatenate([part_re, part_im], axis=1), "freq", scatter_dimension=0, tiled=True
    )
    spec_re = spectrum[:, :width]
    spec_im = spectrum[:, width:]
    stacked = jnp.concatenate([spec_re, spec_im, centroids], axis=0)
    padded = extended(stacked, (("panel", 1),), BLK)
    ext_re = padded[:slab_freqs]
    ext_im = padded[slab_freqs : 2 * slab_freqs]
    ext_xyz = padded[2 * slab_freqs :]
    lap_re, lap_im = laplace(own_freqs)
    out_re, out_im = apply_pairs(
        ext_re, ext_im, ext_xyz, near_list[0], pair_count[0], lap_re, lap_im
    )
    times = jnp.arange(slab_times * lax.axis_size("freq"), dtype=jnp.int32)
    icos, isin = inverse_tables(times, own_freqs)
    return lax.psum_scatter(
        jnp.dot(icos, out_re, precision=highest) - jnp.dot(isin, out_im, precision=highest),
        "freq",
        scatter_dimension=0,
        tiled=True,
    )


def solution(mesh):
    in_specs = (
        P("freq", ("grp", "panel")),
        P(None, ("grp", "panel")),
        P(("grp", "panel"), None, None),
        P(("grp", "panel")),
    )
    out_specs = P("freq", ("grp", "panel"))
    return jax.shard_map(
        per_device, mesh=mesh, in_specs=in_specs, out_specs=out_specs, check_vma=False
    )
```

profile of v0, /device:TPU:0, one launch (start us, length us, event | category | flops | bytes accessed | tf_op | source)
XLA Modules:
  0.0 1480.5 jit_solution(9144158586382741121)
XLA Ops:
  6.6 1.0 copy-done
  7.5 2.8 fusion.30
  10.4 2.8 fusion.34
  13.1 1.3 pad_maximum_fusion
  14.5 0.6 copy-done.3
  15.3 0.5 compare_select_fusion
  15.8 36.8 %reduce-scatter.3.cloned.1.call-done = f32[128,768]{0,1:T(8,128)} async-done(((f32[512,768]{0,1:T(8,128)}), f32[128,768]{0,1:T(8,128)}) %reduce-scatter.3.cloned.1.call-update) | async-done | bytes 393232 | tf_op jit(solution)/shard_map/reduce_scatter | solution.py:106
  52.6 1.0 fusion.71
  53.8 1.7 collective-permute-start.1
  55.5 0.5 iota_add_fusion.1
  56.0 0.6 exponential_multiply_fusion
  56.6 2.5 collective-permute-done
  59.1 0.8 collective-permute-done.1
  60.3 0.4 copy-done.1
  60.7 1029.5 %while.16 = (s32[]{:T(128)}, f32[128,384]{1,0:T(8,128)S(1)}, f32[128,384]{1,0:T(8,128)S(1)}, s32[]{:T(128)}, s32[8,2]{0,1:T(2,128)S(1)}, /*index=5*/f32[3,640]{1...) while((s32[]{:T(128)}, f32[128,384]{1,0:T(8,128)S(1)}, ...), condition=%wide.region_3.4_spmd.clone.clone, body=%wide.region_1.3_spmd.clone.clone.sunk | while | flops 138642832 | bytes 2374013 | solution.py:89
  61.8 0.6 constant_dynamic-slice_fusion.10
  64.1 41.7 %fusion.103 = f32[128,1,128]{2,1,0:T(1,128)S(1)} fusion(f32[128,128,1]{1,2,0:T(1,128)S(1)} %bitcast.61, f32[128]{0:T(128)S(1)} %sine_multiply_fusion.2, f32[128,128]{1,0:T(8,128)S(1)} %get-tuple-element.295, f32[128,128]{1,0:T(8,128)S(1)} %get-tuple-element.296, f32[128]{0:T(128)S(1)} %negate_bitcast_fusion.2), kind=kOutput, calls=%fused_computation.10.clone.1 | convolution fusion | flops 35651584 | bytes 263168 | tf_op jit(solution)/shard_map/while/body/kij,kj->ki/dot_general | solution.py:73
  105.9 41.6 %fusion.102 = f32[128,1,128]{2,1,0:T(1,128)S(1)} fusion(f32[128,128,1]{1,2,0:T(1,128)S(1)} %bitcast.63, f32[128]{0:T(128)S(1)} %sine_multiply_fusion.2, f32[128,128]{1,0:T(8,128)S(1)} %get-tuple-element.295, f32[128,128]{1,0:T(8,128)S(1)} %get-tuple-element.296, f32[128]{0:T(128)S(1)} %negate_bitcast_fusion.2), kind=kOutput, calls=%fused_computation.8.clone.1 | convolution fusion | flops 33554432 | bytes 263168 | tf_op jit(solution)/shard_map/while/body/kij,kj->ki/dot_general | solution.py:73
  147.5 41.9 %fusion.101 = f32[128,1,128]{2,1,0:T(1,128)S(1)} fusion(f32[128,128,1]{1,2,0:T(1,128)S(1)} %bitcast.64, f32[128]{0:T(128)S(1)} %sine_multiply_fusion.2, f32[128,128]{1,0:T(8,128)S(1)} %get-tuple-element.295, f32[128,128]{1,0:T(8,128)S(1)} %get-tuple-element.296, f32[128]{0:T(128)S(1)} %negate_bitcast_fusion.2), kind=kOutput, calls=%fused_computation.9.clone.1 | convolution fusion | flops 35651584 | bytes 263168 | tf_op jit(solution)/shard_map/while/body/kij,kj->ki/dot_general | solution.py:76
  189.4 41.4 %fusion.100 = f32[128,1,128]{2,1,0:T(1,128)S(1)} fusion(f32[128,128,1]{1,2,0:T(1,128)S(1)} %bitcast.62, f32[128]{0:T(128)S(1)} %sine_multiply_fusion.2, f32[128,128]{1,0:T(8,128)S(1)} %get-tuple-element.295, f32[128,128]{1,0:T(8,128)S(1)} %get-tuple-element.296, f32[128]{0:T(128)S(1)} %negate_bitcast_fusion.2), kind=kOutput, calls=%fused_computation.7.clone.1 | convolution fusion | flops 33554432 | bytes 263168 | tf_op jit(solution)/shard_map/while/body/kij,kj->ki/dot_general | solution.py:76
  232.5 0.6 constant_dynamic-slice_fusion.10
  234.8 41.7 %fusion.103 = f32[128,1,128]{2,1,0:T(1,128)S(1)} fusion(f32[128,128,1]{1,2,0:T(1,128)S(1)} %bitcast.61, f32[128]{0:T(128)S(1)} %sine_multiply_fusion.2, f32[128,128]{1,0:T(8,128)S(1)} %get-tuple-element.295, f32[128,128]{1,0:T(8,128)S(1)} %get-tuple-element.296, f32[128]{0:T(128)S(1)} %negate_bitcast_fusion.2), kind=kOutput, calls=%fused_computation.10.clone.1 | convolution fusion | flops 35651584 | bytes 263168 | tf_op jit(solution)/shard_map/while/body/kij,kj->ki/dot_general | solution.py:73
  276.7 41.3 %fusion.102 = f32[128,1,128]{2,1,0:T(1,128)S(1)} fusion(f32[128,128,1]{1,2,0:T(1,128)S(1)} %bitcast.63, f32[128]{0:T(128)S(1)} %sine_multiply_fusion.2, f32[128,128]{1,0:T(8,128)S(1)} %get-tuple-element.295, f32[128,128]{1,0:T(8,128)S(1)} %get-tuple-element.296, f32[128]{0:T(128)S(1)} %negate_bitcast_fusion.2), kind=kOutput, calls=%fused_computation.8.clone.1 | convolution fusion | flops 33554432 | bytes 263168 | tf_op jit(solution)/shard_map/while/body/kij,kj->ki/dot_general | solution.py:73
  318.0 41.9 %fusion.101 = f32[128,1,128]{2,1,0:T(1,128)S(1)} fusion(f32[128,128,1]{1,2,0:T(1,128)S(1)} %bitcast.64, f32[128]{0:T(128)S(1)} %sine_multiply_fusion.2, f32[128,128]{1,0:T(8,128)S(1)} %get-tuple-element.295, f32[128,128]{1,0:T(8,128)S(1)} %get-tuple-element.296, f32[128]{0:T(128)S(1)} %negate_bitcast_fusion.2), kind=kOutput, calls=%fused_computation.9.clone.1 | convolution fusion | flops 35651584 | bytes 263168 | tf_op jit(solution)/shard_map/while/body/kij,kj->ki/dot_general | solution.py:76
  359.9 41.6 %fusion.100 = f32[128,1,128]{2,1,0:T(1,128)S(1)} fusion(f32[128,128,1]{1,2,0:T(1,128)S(1)} %bitcast.62, f32[128]{0:T(128)S(1)} %sine_multiply_fusion.2, f32[128,128]{1,0:T(8,128)S(1)} %get-tuple-element.295, f32[128,128]{1,0:T(8,128)S(1)} %get-tuple-element.296, f32[128]{0:T(128)S(1)} %negate_bitcast_fusion.2), kind=kOutput, calls=%fused_computation.7.clone.1 | convolution fusion | flops 33554432 | bytes 263168 | tf_op jit(solution)/shard_map/while/body/kij,kj->ki/dot_general | solution.py:76
  403.0 0.6 constant_dynamic-slice_fusion.10
  405.3 41.7 %fusion.103 = f32[128,1,128]{2,1,0:T(1,128)S(1)} fusion(f32[128,128,1]{1,2,0:T(1,128)S(1)} %bitcast.61, f32[128]{0:T(128)S(1)} %sine_multiply_fusion.2, f32[128,128]{1,0:T(8,128)S(1)} %get-tuple-element.295, f32[128,128]{1,0:T(8,128)S(1)} %get-tuple-element.296, f32[128]{0:T(128)S(1)} %negate_bitcast_fusion.2), kind=kOutput, calls=%fused_computation.10.clone.1 | convolution fusion | flops 35651584 | bytes 263168 | tf_op jit(solution)/shard_map/while/body/kij,kj->ki/dot_general | solution.py:73
  447.1 41.4 %fusion.102 = f32[128,1,128]{2,1,0:T(1,128)S(1)} fusion(f32[128,128,1]{1,2,0:T(1,128)S(1)} %bitcast.63, f32[128]{0:T(128)S(1)} %sine_multiply_fusion.2, f32[128,128]{1,0:T(8,128)S(1)} %get-tuple-element.295, f32[128,128]{1,0:T(8,128)S(1)} %get-tuple-element.296, f32[128]{0:T(128)S(1)} %negate_bitcast_fusion.2), kind=kOutput, calls=%fused_computation.8.clone.1 | convolution fusion | flops 33554432 | bytes 263168 | tf_op jit(solution)/shard_map/while/body/kij,kj->ki/dot_general | solution.py:73
  488.5 42.1 %fusion.101 = f32[128,1,128]{2,1,0:T(1,128)S(1)} fusion(f32[128,128,1]{1,2,0:T(1,128)S(1)} %bitcast.64, f32[128]{0:T(128)S(1)} %sine_multiply_fusion.2, f32[128,128]{1,0:T(8,128)S(1)} %get-tuple-element.295, f32[128,128]{1,0:T(8,128)S(1)} %get-tuple-element.296, f32[128]{0:T(128)S(1)} %negate_bitcast_fusion.2), kind=kOutput, calls=%fused_computation.9.clone.1 | convolution fusion | flops 35651584 | bytes 263168 | tf_op jit(solution)/shard_map/while/body/kij,kj->ki/dot_general | solution.py:76
  530.6 41.3 %fusion.100 = f32[128,1,128]{2,1,0:T(1,128)S(1)} fusion(f32[128,128,1]{1,2,0:T(1,128)S(1)} %bitcast.62, f32[128]{0:T(128)S(1)} %sine_multiply_fusion.2, f32[128,128]{1,0:T(8,128)S(1)} %get-tuple-element.295, f32[128,128]{1,0:T(8,128)S(1)} %get-tuple-element.296, f32[128]{0:T(128)S(1)} %negate_bitcast_fusion.2), kind=kOutput, calls=%fused_computation.7.clone.1 | convolution fusion | flops 33554432 | bytes 263168 | tf_op jit(solution)/shard_map/while/body/kij,kj->ki/dot_general | solution.py:76
  573.6 0.6 constant_dynamic-slice_fusion.10
  575.9 41.7 %fusion.103 = f32[128,1,128]{2,1,0:T(1,128)S(1)} fusion(f32[128,128,1]{1,2,0:T(1,128)S(1)} %bitcast.61, f32[128]{0:T(128)S(1)} %sine_multiply_fusion.2, f32[128,128]{1,0:T(8,128)S(1)} %get-tuple-element.295, f32[128,128]{1,0:T(8,128)S(1)} %get-tuple-element.296, f32[128]{0:T(128)S(1)} %negate_bitcast_fusion.2), kind=kOutput, calls=%fused_computation.10.clone.1 | convolution fusion | flops 35651584 | bytes 263168 | tf_op jit(solution)/shard_map/while/body/kij,kj->ki/dot_general | solution.py:73
  617.7 41.6 %fusion.102 = f32[128,1,128]{2,1,0:T(1,128)S(1)} fusion(f32[128,128,1]{1,2,0:T(1,128)S(1)} %bitcast.63, f32[128]{0:T(128)S(1)} %sine_multiply_fusion.2, f32[128,128]{1,0:T(8,128)S(1)} %get-tuple-element.295, f32[128,128]{1,0:T(8,128)S(1)} %get-tuple-element.296, f32[128]{0:T(128)S(1)} %negate_bitcast_fusion.2), kind=kOutput, calls=%fused_computation.8.clone.1 | convolution fusion | flops 33554432 | bytes 263168 | tf_op jit(solution)/shard_map/while/body/kij,kj->ki/dot_general | solution.py:73
  659.3 41.9 %fusion.101 = f32[128,1,128]{2,1,0:T(1,128)S(1)} fusion(f32[128,128,1]{1,2,0:T(1,128)S(1)} %bitcast.64, f32[128]{0:T(128)S(1)} %sine_multiply_fusion.2, f32[128,128]{1,0:T(8,128)S(1)} %get-tuple-element.295, f32[128,128]{1,0:T(8,128)S(1)} %get-tuple-element.296, f32[128]{0:T(128)S(1)} %negate_bitcast_fusion.2), kind=kOutput, calls=%fused_computation.9.clone.1 | convolution fusion | flops 35651584 | bytes 263168 | tf_op jit(solution)/shard_map/while/body/kij,kj->ki/dot_general | solution.py:76
  701.1 41.4 %fusion.100 = f32[128,1,128]{2,1,0:T(1,128)S(1)} fusion(f32[128,128,1]{1,2,0:T(1,128)S(1)} %bitcast.62, f32[128]{0:T(128)S(1)} %sine_multiply_fusion.2, f32[128,128]{1,0:T(8,128)S(1)} %get-tuple-element.295, f32[128,128]{1,0:T(8,128)S(1)} %get-tuple-element.296, f32[128]{0:T(128)S(1)} %negate_bitcast_fusion.2), kind=kOutput, calls=%fused_computation.7.clone.1 | convolution fusion | flops 33554432 | bytes 263168 | tf_op jit(solution)/shard_map/while/body/kij,kj->ki/dot_general | solution.py:76
  744.3 0.6 constant_dynamic-slice_fusion.10
  746.6 41.7 %fusion.103 = f32[128,1,128]{2,1,0:T(1,128)S(1)} fusion(f32[128,128,1]{1,2,0:T(1,128)S(1)} %bitcast.61, f32[128]{0:T(128)S(1)} %sine_multiply_fusion.2, f32[128,128]{1,0:T(8,128)S(1)} %get-tuple-element.295, f32[128,128]{1,0:T(8,128)S(1)} %get-tuple-element.296, f32[128]{0:T(128)S(1)} %negate_bitcast_fusion.2), kind=kOutput, calls=%fused_computation.10.clone.1 | convolution fusion | flops 35651584 | bytes 263168 | tf_op jit(solution)/shard_map/while/body/kij,kj->ki/dot_general | solution.py:73
  788.4 41.3 %fusion.102 = f32[128,1,128]{2,1,0:T(1,128)S(1)} fusion(f32[128,128,1]{1,2,0:T(1,128)S(1)} %bitcast.63, f32[128]{0:T(128)S(1)} %sine_multiply_fusion.2, f32[128,128]{1,0:T(8,128)S(1)} %get-tuple-element.295, f32[128,128]{1,0:T(8,128)S(1)} %get-tuple-element.296, f32[128]{0:T(128)S(1)} %negate_bitcast_fusion.2), kind=kOutput, calls=%fused_computation.8.clone.1 | convolution fusion | flops 33554432 | bytes 263168 | tf_op jit(solution)/shard_map/while/body/kij,kj->ki/dot_general | solution.py:73
  829.7 41.9 %fusion.101 = f32[128,1,128]{2,1,0:T(1,128)S(1)} fusion(f32[128,128,1]{1,2,0:T(1,128)S(1)} %bitcast.64, f32[128]{0:T(128)S(1)} %sine_multiply_fusion.2, f32[128,128]{1,0:T(8,128)S(1)} %get-tuple-element.295, f32[128,128]{1,0:T(8,128)S(1)} %get-tuple-element.296, f32[128]{0:T(128)S(1)} %negate_bitcast_fusion.2), kind=kOutput, calls=%fused_computation.9.clone.1 | convolution fusion | flops 35651584 | bytes 263168 | tf_op jit(solution)/shard_map/while/body/kij,kj->ki/dot_general | solution.py:76
  871.6 41.6 %fusion.100 = f32[128,1,128]{2,1,0:T(1,128)S(1)} fusion(f32[128,128,1]{1,2,0:T(1,128)S(1)} %bitcast.62, f32[128]{0:T(128)S(1)} %sine_multiply_fusion.2, f32[128,128]{1,0:T(8,128)S(1)} %get-tuple-element.295, f32[128,128]{1,0:T(8,128)S(1)} %get-tuple-element.296, f32[128]{0:T(128)S(1)} %negate_bitcast_fusion.2), kind=kOutput, calls=%fused_computation.7.clone.1 | convolution fusion | flops 33554432 | bytes 263168 | tf_op jit(solution)/shard_map/while/body/kij,kj->ki/dot_general | solution.py:76
  914.8 0.6 constant_dynamic-slice_fusion.10
  917.1 41.7 %fusion.103 = f32[128,1,128]{2,1,0:T(1,128)S(1)} fusion(f32[128,128,1]{1,2,0:T(1,128)S(1)} %bitcast.61, f32[128]{0:T(128)S(1)} %sine_multiply_fusion.2, f32[128,128]{1,0:T(8,128)S(1)} %get-tuple-element.295, f32[128,128]{1,0:T(8,128)S(1)} %get-tuple-element.296, f32[128]{0:T(128)S(1)} %negate_bitcast_fusion.2), kind=kOutput, calls=%fused_computation.10.clone.1 | convolution fusion | flops 35651584 | bytes 263168 | tf_op jit(solution)/shard_map/while/body/kij,kj->ki/dot_general | solution.py:73
  958.9 41.4 %fusion.102 = f32[128,1,128]{2,1,0:T(1,128)S(1)} fusion(f32[128,128,1]{1,2,0:T(1,128)S(1)} %bitcast.63, f32[128]{0:T(128)S(1)} %sine_multiply_fusion.2, f32[128,128]{1,0:T(8,128)S(1)} %get-tuple-element.295, f32[128,128]{1,0:T(8,128)S(1)} %get-tuple-element.296, f32[128]{0:T(128)S(1)} %negate_bitcast_fusion.2), kind=kOutput, calls=%fused_computation.8.clone.1 | convolution fusion | flops 33554432 | bytes 263168 | tf_op jit(solution)/shard_map/while/body/kij,kj->ki/dot_general | solution.py:73
  1000.3 42.1 %fusion.101 = f32[128,1,128]{2,1,0:T(1,128)S(1)} fusion(f32[128,128,1]{1,2,0:T(1,128)S(1)} %bitcast.64, f32[128]{0:T(128)S(1)} %sine_multiply_fusion.2, f32[128,128]{1,0:T(8,128)S(1)} %get-tuple-element.295, f32[128,128]{1,0:T(8,128)S(1)} %get-tuple-element.296, f32[128]{0:T(128)S(1)} %negate_bitcast_fusion.2), kind=kOutput, calls=%fused_computation.9.clone.1 | convolution fusion | flops 35651584 | bytes 263168 | tf_op jit(solution)/shard_map/while/body/kij,kj->ki/dot_general | solution.py:76
  1042.4 41.3 %fusion.100 = f32[128,1,128]{2,1,0:T(1,128)S(1)} fusion(f32[128,128,1]{1,2,0:T(1,128)S(1)} %bitcast.62, f32[128]{0:T(128)S(1)} %sine_multiply_fusion.2, f32[128,128]{1,0:T(8,128)S(1)} %get-tuple-element.295, f32[128,128]{1,0:T(8,128)S(1)} %get-tuple-element.296, f32[128]{0:T(128)S(1)} %negate_bitcast_fusion.2), kind=kOutput, calls=%fused_computation.7.clone.1 | convolution fusion | flops 33554432 | bytes 263168 | tf_op jit(solution)/shard_map/while/body/kij,kj->ki/dot_general | solution.py:76
  1090.2 3.3 fusion.22
  1093.5 4.6 convolution_subtract_fusion
  1098.2 375.2 %reduce-scatter.5.cloned.1.call-done = f32[256,384]{1,0:T(8,128)} async-done(((f32[1024,384]{1,0:T(8,128)}), f32[256,384]{1,0:T(8,128)}) %reduce-scatter.5.cloned.1.call-update) | async-done | bytes 393232 | tf_op jit(solution)/shard_map/reduce_scatter | solution.py:122
  (84 shorter events, 3.6 us)
Async XLA Ops:
  6.5 1.0 copy-start
  6.5 46.1 %reduce-scatter.3.cloned.1.call-start = ((), (), s32[]{:S(2)}) async-start(), calls=%async_computation.2 | async-start | bytes 1966080 | tf_op jit(solution)/shard_map/reduce_scatter | solution.py:106
  14.5 0.7 copy-start.3
  14.5 1458.8 %reduce-scatter.5.cloned.1.call-start = ((), (), s32[]{:S(2)}) async-start(), calls=%async_computation.3 | async-start | bytes 1966080 | tf_op jit(solution)/shard_map/reduce_scatter | solution.py:122
  53.7 5.4 collective-permute-start
  53.8 6.2 collective-permute-start.1
  60.0 0.7 copy-start.1
  60.7 1029.5 %copy-start.2 = (f32[1024]{0:T(1024)S(1)}, f32[1024]{0:T(1024)}, u32[]{:S(2)}) copy-start(f32[1024]{0:T(1024)} %exponential_multiply_fusion) | copy-start | bytes 12292
  60.7 1029.5 %copy-start.4 = (f32[128]{0:T(128)S(1)}, f32[128]{0:T(128)}, u32[]{:S(2)}) copy-start(f32[128]{0:T(128)} %compare_select_fusion) | copy-start | bytes 1540
  60.7 1029.5 %copy-start.5 = (s32[128]{0:T(128)S(1)}, s32[128]{0:T(128)}, u32[]{:S(2)}) copy-start(s32[128]{0:T(128)} %iota_add_fusion.1) | copy-start | bytes 1540
Sparse Core Ops, SparseCore 0:
  14.6 37.9 reduce-scatter.2
  1098.3 374.9 reduce-scatter.4
where the time goes:
time: 1490 us; the launch traced here: 1480 us
  matrix products  1010 us (68%)
  waiting for transfers between devices  415 us (28%)
  loops' own time  23.5 us (2%)
    reduce_scatter x1, waiting for transfers between devices, per_device(): lax.psum_scatter(jnp.dot(icos, out_re, precision=highest) - jnp.dot(isin,...  375 us
    dot_general x6, matrix products, add_pair(): jnp.einsum('kij,kj->ki', k_im, g_re, precision=highest)  252 us
    dot_general x6, matrix products, add_pair(): jnp.einsum('kij,kj->ki', k_im, g_im, precision=highest)  250 us
    dot_general x6, matrix products, add_pair(): jnp.einsum('kij,kj->ki', k_re, g_re, precision=highest)  249 us
    dot_general x6, matrix products, add_pair(): jnp.einsum('kij,kj->ki', k_re, g_im, precision=highest)  249 us
    reduce_scatter x1, waiting for transfers between devices, per_device(): lax.psum_scatter(jnp.concatenate([part_re, part_im], axis=1), 'freq', sca...  36.8 us
  transfers between devices with their start and end apart: 4, of which 4 were waited for; matrix products, arithmetic and copies ran while one was open for 0% of the time, Pallas kernels for 0%

commit v1 on v0

v1 whole, which is shorter than its diff:
```python
import math

import jax
import jax.numpy as jnp
from jax import lax
from jax.experimental import pallas as pl
from jax.experimental.pallas import tpu as pltpu
from jax.sharding import PartitionSpec as P

NT = 1024
BLK = 128
TAPS = 32
HALF = TAPS // 2
GEO = 8

damping = 0.999
time_step = 0.5
core_square = 0.01


def split(v):
    hi = v.astype(jnp.bfloat16)
    return hi, (v - hi.astype(jnp.float32)).astype(jnp.bfloat16)


def near_field(list_ref, count_ref, slab_ref, ext_ref, out_ref, shifted, coeffs, turned, acc, last):
    steps = out_ref.shape[0]
    blocks = acc.shape[0]
    geo = TAPS + steps
    for c in range(blocks + 2):
        for n in range(HALF):
            hi, lo = split(ext_ref[c, HALF - n : HALF - n + steps + HALF, :])
            shifted[c, 0, :, n * BLK : (n + 1) * BLK] = hi
            shifted[c, 1, :, n * BLK : (n + 1) * BLK] = lo
        rows = ext_ref[c, geo : geo + GEO, :]
        turned[c] = jnp.concatenate([rows] * (BLK // GEO), axis=0).T
    acc[...] = jnp.zeros_like(acc)
    last[...] = jnp.zeros_like(last)

    def add_pair(slot, carry):
        row = list_ref[slot, 0]
        col = list_ref[slot, 1]
        mine = ext_ref[row + 1, geo : geo + GEO, :]
        theirs = turned[col]
        square = jnp.full((BLK, BLK), core_square, jnp.float32)
        for a in range(3):
            diff = theirs[:, a : a + 1] - mine[a : a + 1, :]
            square = square + diff * diff
        dist = jnp.sqrt(square)
        x = dist * (1.0 / time_step)
        term = jnp.exp(-x) / (4.0 * math.pi * dist)
        nyquist = term * jnp.exp(-damping * x) * theirs[:, 3:4]
        last[row] = last[row] + jnp.sum(nyquist, axis=0, keepdims=True)
        for n in range(TAPS):
            hi, lo = split(term)
            coeffs[n * BLK : (n + 1) * BLK, :BLK] = hi
            coeffs[n * BLK : (n + 1) * BLK, BLK:] = lo
            term = term * (x * (1.0 / (n + 1)))
        near = coeffs[: HALF * BLK, :]
        far = coeffs[HALF * BLK :, :]
        total = acc[row]
        for part in range(2):
            both = jnp.dot(
                shifted[col, part, HALF:, :], near, preferred_element_type=jnp.float32
            ) + jnp.dot(
                shifted[col, part, :steps, :], far, preferred_element_type=jnp.float32
            )
            total = total + (both[:, :BLK] + both[:, BLK:])
        acc[row] = total
        return carry

    lax.fori_loop(0, count_ref[0], add_pair, 0)
    local = lax.broadcasted_iota(jnp.int32, (steps, BLK), 0)
    times = (slab_ref[0] * steps + local).astype(jnp.float32)
    growth = jnp.exp(-times * math.log(damping)) / NT
    growth = jnp.where(local % 2 == 0, growth, -growth)
    for r in range(blocks):
        out_ref[:, r * BLK : (r + 1) * BLK] = acc[r] - growth * last[r, 0:1, :]


def per_device(traces, centroids, near_list, pair_count):
    steps, width = traces.shape
    blocks = width // BLK
    groups = lax.axis_size("freq")
    shards = lax.axis_size("panel")
    position = lax.axis_index("freq")
    halo = lax.ppermute(
        traces[steps - TAPS :], "freq", [(i, (i + 1) % groups) for i in range(groups)]
    )
    halo = halo * jnp.where(position == 0, math.exp(NT * math.log(damping)), 1.0)
    times = position * steps + jnp.arange(steps, dtype=jnp.int32)
    weight = jnp.exp(times.astype(jnp.float32) * math.log(damping))
    weight = jnp.where(times % 2 == 0, weight, -weight)
    nyquist = lax.psum(jnp.sum(weight[:, None] * traces, axis=0, keepdims=True), "freq")
    pad = jnp.zeros((GEO - 4, width), jnp.float32)
    own = jnp.concatenate([halo, traces, centroids, nyquist, pad], axis=0)
    up = [(i, (i + 1) % shards) for i in range(shards)]
    before = lax.ppermute(own[:, width - BLK :], "panel", up)
    after = lax.ppermute(own[:, :BLK], "panel", [(j, i) for i, j in up])
    pieces = [before] + [own[:, r * BLK : (r + 1) * BLK] for r in range(blocks)] + [after]
    ext = jnp.stack(pieces, axis=0)
    smem = pl.BlockSpec(memory_space=pltpu.SMEM)
    return pl.pallas_call(
        near_field,
        out_shape=jax.ShapeDtypeStruct((steps, width), jnp.float32),
        in_specs=[smem, smem, smem, pl.BlockSpec(memory_space=pltpu.VMEM)],
        out_specs=pl.BlockSpec(memory_space=pltpu.VMEM),
        scratch_shapes=[
            pltpu.VMEM((blocks + 2, 2, steps + HALF, HALF * BLK), jnp.bfloat16),
            pltpu.VMEM((TAPS * BLK, 2 * BLK), jnp.bfloat16),
            pltpu.VMEM((blocks + 2, BLK, BLK), jnp.float32),
            pltpu.VMEM((blocks, steps, BLK), jnp.float32),
            pltpu.VMEM((blocks, 8, BLK), jnp.float32),
        ],
        compiler_params=pltpu.CompilerParams(vmem_limit_bytes=40 * 1024 * 1024),
    )(near_list[0], pair_count, position.reshape(1).astype(jnp.int32), ext)


def solution(mesh):
    in_specs = (
        P("freq", ("grp", "panel")),
        P(None, ("grp", "panel")),
        P(("grp", "panel"), None, None),
        P(("grp", "panel")),
    )
    out_specs = P("freq", ("grp", "panel"))
    return jax.shard_map(
        per_device, mesh=mesh, in_specs=in_specs, out_specs=out_specs, check_vma=False
    )
```

time: 1490 us -> 40.6 us (0.03)
  matrix products: 1010 us -> 0 us
  waiting for transfers between devices: 415 us -> 2.86 us
  loops' own time: 23.5 us -> 0 us
  Pallas kernels: 0 us -> 18 us
    dot_general x28 -> x0, matrix products: 1010 us -> none  [the longest x6 252 us: add_pair(): jnp.einsum('kij,kj->ki', k_im, g_re, precision=highest)]
    reduce_scatter x2 -> x0, waiting for transfers between devices: 412 us -> none  [the longest x1 375 us: per_device(): lax.psum_scatter(jnp.dot(icos, out_re, precision=highest) - jnp.dot(isin,...]
    another operation x1 -> x0, loops' own time: 23.5 us -> none  [apply_pairs(): return lax.fori_loop(jnp.int32(0), count, add_pair, (zeros, zeros))]
    pallas_call x0 -> x1, Pallas kernels: none -> 18 us  [per_device(): pl.pallas_call(near_field, out_shape=jax.ShapeDtypeStruct((steps, width),...]
  transfers between devices with their start and end apart: 4 -> 3, of which waited for: 4 -> 2; matrix products, arithmetic and copies ran while one was open for 0% -> 3% of each run, Pallas kernels for 0% -> 0%
where the time goes in v1:
time: 40.6 us; the launch traced here: 39.8 us
  Pallas kernels  18 us (44%)
  blocking collectives  10.4 us (26%)
  starting transfers between devices  4.26 us (10%)
  waiting for transfers between devices  2.86 us (7%)
  local copies, waits for them, and re-layouts  2.45 us (6%)
  other arithmetic  1.13 us (3%)
  between operations  0.76 us (2%)
    pallas_call x1, Pallas kernels, per_device(): pl.pallas_call(near_field, out_shape=jax.ShapeDtypeStruct((steps, width),...  18 us
    psum x1, blocking collectives, per_device(): lax.psum(jnp.sum(weight[:, None] * traces, axis=0, keepdims=True), 'freq')  10.4 us
    ppermute x1, starting transfers between devices, per_device(): lax.ppermute(traces[steps - TAPS:], 'freq', [(i, (i + 1) % groups) for i...  3.02 us
    ppermute x1, waiting for transfers between devices, per_device(): before = lax.ppermute(own[:, width - BLK:], 'panel', up)  2.08 us
    unnamed x10, local copies, waits for them, and re-layouts  1.33 us
    ppermute x1, starting transfers between devices, per_device(): after = lax.ppermute(own[:, :BLK], 'panel', [(j, i) for i, j in up])  1.18 us
    reduce_sum x1, other arithmetic, per_device(): jnp.sum(weight[:, None] * traces, axis=0, keepdims=True)  1.11 us
    slice x1, local copies, waits for them, and re-layouts, per_device(): traces[steps - TAPS:]  0.87 us
  transfers between devices with their start and end apart: 3, of which 2 were waited for; matrix products, arithmetic and copies ran while one was open for 3% of the time, Pallas kernels for 0%

profile of v1, /device:TPU:0, one launch (start us, length us, event | category | flops | bytes accessed | tf_op | source)
XLA Modules:
  0.0 39.8 jit_solution(9077472612174717437)
XLA Ops:
  0.0 0.0 copy-start
  0.0 0.9 %slice.14 = f32[32,384]{1,0:T(8,128)S(1)} slice(f32[256,384]{1,0:T(8,128)} %param.4), slice={[224:256], [0:384]} | slice | bytes 98304 | tf_op jit(solution)/shard_map/slice | solution.py:88
  0.9 3.0 %collective-permute-start = (f32[32,384]{1,0:T(8,128)S(1)}, f32[32,384]{1,0:T(8,128)S(1)}, u32[]{:S(2)}, u32[]{:S(2)}) collective-permute-start(f32[32,384]{1,0:T(8,128)S(1)} %slice.14), channel_id=1, source_target_pairs={{0,4},{4,8},{8,12},{12,0},{1,5},{5,9},{9,13},{13,1},{2,6},{6,10},{... | collective-permute-start | bytes 147464 | tf_op jit(solution)/shard_map/ppermute | solution.py:87
  3.9 1.1 %multiply_reduce_fusion = f32[384]{0:T(512)S(1)} fusion(f32[256,384]{1,0:T(8,128)} %param.4, f32[256]{0:T(256)S(1)} %compare_select_fusion.2), kind=kLoop, calls=%fused_computation | loop fusion | flops 196224 | bytes 395776 | tf_op jit(solution)/shard_map/reduce_sum | solution.py:94
  5.0 10.4 %psum.7 = f32[1,384]{1,0:T(1,128)S(1)} all-reduce(f32[1,384]{1,0:T(1,128)S(1)} %broadcast_in_dim.7), channel_id=1, replica_groups=mesh['grp'=2,'freq'=4,'panel'=4] {'freq'}, use_global_device_ids=true, to_apply=%region_1.2 | all-reduce | flops 384 | bytes 3072 | tf_op jit(solution)/shard_map/psum | solution.py:94
  15.4 0.0 collective-permute-done
  15.5 0.0 copy-start.1
  15.5 0.0 copy-done
  15.5 0.7 %copy-done.1 = f32[3,384]{1,0:T(4,128)S(1)} copy-done((f32[3,384]{1,0:T(4,128)S(1)}, f32[3,384]{1,0:T(4,128)}, u32[]{:S(2)}) %copy-start.1) | copy-done | bytes 4632
  16.1 0.1 concatenate.3
  16.3 0.0 copy-start.2
  16.3 0.1 collective-permute-start.1
  16.4 0.6 %copy-done.2 = s32[1,8,2]{1,2,0:T(2,128)S(1)} copy-done((s32[1,8,2]{1,2,0:T(2,128)S(1)}, s32[1,8,2]{1,2,0:T(2,128)}, u32[]{:S(2)}) %copy-start.2) | copy-done | bytes 88
  17.0 0.1 copy.5.list_ref
  17.7 1.2 %collective-permute-start.2 = (f32[296,128]{1,0:T(8,128)S(1)}, f32[296,128]{1,0:T(8,128)S(1)}, u32[]{:S(2)}, u32[]{:S(2)}) collective-permute-start(f32[296,128]{1,0:T(8,128)S(1)} %get-tuple-element.5), channel_id=1, source_target_pairs={{1,0},{2,1},{3,2},{0,3},{5,4},{6,5},{7,6},{4,7},{9,8},{10,9},{11,1... | collective-permute-start | bytes 454664 | tf_op jit(solution)/shard_map/ppermute | solution.py:99
  18.9 2.1 %collective-permute-done.1 = f32[296,128]{1,0:T(8,128)S(1)} collective-permute-done((f32[296,128]{1,0:T(8,128)S(1)}, f32[296,128]{1,0:T(8,128)S(1)}, u32[]{:S(2)}, u32[]{:S(2)}) %collective-permute-start.1) | collective-permute-done | bytes 151584 | tf_op jit(solution)/shard_map/ppermute | solution.py:98
  21.1 0.8 %collective-permute-done.2 = f32[296,128]{1,0:T(8,128)S(1)} collective-permute-done((f32[296,128]{1,0:T(8,128)S(1)}, f32[296,128]{1,0:T(8,128)S(1)}, u32[]{:S(2)}, u32[]{:S(2)}) %collective-permute-start.2) | collective-permute-done | bytes 151584 | tf_op jit(solution)/shard_map/ppermute | solution.py:99
  21.8 18.0 %shard_map.46 = f32[256,384]{1,0:T(8,128)} custom-call(s32[8,2]{1,0:T(8,128)S(1)} %copy.5.list_ref, s32[1]{0:T(128)S(6)} %copy.10.count_ref, s32[1]{0:T(128)} %bitcast.1.slab_ref, f32[5,296,128]{2,1,0:T(8,128)S(1)} %bitcast_dynamic-update-slice_fusion.ext_ref), custom_call_target="tpu_custom_call" | custom-call | tf_op jit(solution)/shard_map/pallas_call | solution.py:103
  (10 shorter events, 0.1 us)
Async XLA Ops:
  0.0 15.5 %copy-start = (f32[256,384]{1,0:T(8,128)S(1)}, f32[256,384]{1,0:T(8,128)}, u32[]{:S(2)}) copy-start(f32[256,384]{1,0:T(8,128)} %param.4) | copy-start | bytes 1179652
  0.9 14.6 %collective-permute-start = (f32[32,384]{1,0:T(8,128)S(1)}, f32[32,384]{1,0:T(8,128)S(1)}, u32[]{:S(2)}, u32[]{:S(2)}) collective-permute-start(f32[32,384]{1,0:T(8,128)S(1)} %slice.14), channel_id=1, source_target_pairs={{0,4},{4,8},{8,12},{12,0},{1,5},{5,9},{9,13},{13,1},{2,6},{6,10},{... | collective-permute-start | bytes 147464 | tf_op jit(solution)/shard_map/ppermute | solution.py:87
  15.5 0.7 %copy-start.1 = (f32[3,384]{1,0:T(4,128)S(1)}, f32[3,384]{1,0:T(4,128)}, u32[]{:S(2)}) copy-start(f32[3,384]{1,0:T(4,128)} %param.5) | copy-start | bytes 13828
  16.3 0.7 %copy-start.2 = (s32[1,8,2]{1,2,0:T(2,128)S(1)}, s32[1,8,2]{1,2,0:T(2,128)}, u32[]{:S(2)}) copy-start(s32[1,8,2]{1,2,0:T(2,128)} %param.6) | copy-start | bytes 196
  16.3 4.7 %collective-permute-start.1 = (f32[296,128]{1,0:T(8,128)S(1)}, f32[296,128]{1,0:T(8,128)S(1)}, u32[]{:S(2)}, u32[]{:S(2)}) collective-permute-start(f32[296,128]{1,0:T(8,128)S(1)} %get-tuple-element.6), channel_id=1, source_target_pairs={{0,1},{1,2},{2,3},{3,0},{4,5},{5,6},{6,7},{7,4},{8,9},{9,10},{10,1... | collective-permute-start | bytes 454664 | tf_op jit(solution)/shard_map/ppermute | solution.py:98
  17.7 4.1 %collective-permute-start.2 = (f32[296,128]{1,0:T(8,128)S(1)}, f32[296,128]{1,0:T(8,128)S(1)}, u32[]{:S(2)}, u32[]{:S(2)}) collective-permute-start(f32[296,128]{1,0:T(8,128)S(1)} %get-tuple-element.5), channel_id=1, source_target_pairs={{1,0},{2,1},{3,2},{0,3},{5,4},{6,5},{7,6},{4,7},{9,8},{10,9},{11,1... | collective-permute-start | bytes 454664 | tf_op jit(solution)/shard_map/ppermute | solution.py:99

commit v2 on v1

--- a/solution.py
+++ b/solution.py
@@ -23,7 +23,9 @@
     return hi, (v - hi.astype(jnp.float32)).astype(jnp.bfloat16)
 
 
-def near_field(list_ref, count_ref, slab_ref, ext_ref, out_ref, shifted, coeffs, turned, acc, last):
+def near_field(
+    list_ref, count_ref, slab_ref, ext_ref, nyquist_ref, out_ref, shifted, coeffs, turned, acc, last
+):
     steps = out_ref.shape[0]
     blocks = acc.shape[0]
     geo = TAPS + steps
@@ -32,7 +34,9 @@
             hi, lo = split(ext_ref[c, HALF - n : HALF - n + steps + HALF, :])
             shifted[c, 0, :, n * BLK : (n + 1) * BLK] = hi
             shifted[c, 1, :, n * BLK : (n + 1) * BLK] = lo
-        rows = ext_ref[c, geo : geo + GEO, :]
+        place = lax.broadcasted_iota(jnp.int32, (GEO, BLK), 0)
+        sample = jnp.sum(nyquist_ref[c], axis=0, keepdims=True)
+        rows = jnp.where(place == 3, sample, ext_ref[c, geo : geo + GEO, :])
         turned[c] = jnp.concatenate([rows] * (BLK // GEO), axis=0).T
     acc[...] = jnp.zeros_like(acc)
     last[...] = jnp.zeros_like(last)
@@ -78,33 +82,108 @@
         out_ref[:, r * BLK : (r + 1) * BLK] = acc[r] - growth * last[r, 0:1, :]
 
 
+def exchange(traces_ref, xyz_ref, ext_ref, nyquist_ref, parts, slots, send, recv):
+    steps, width = traces_ref.shape
+    blocks = width // BLK
+    geo = TAPS + steps
+    groups = lax.axis_size("freq")
+    shards = lax.axis_size("panel")
+    position = lax.axis_index("freq")
+    shard = lax.axis_index("panel")
+
+    def device(ahead, side):
+        return {
+            "freq": lax.rem(position + ahead, groups),
+            "panel": lax.rem(shard + side + shards, shards),
+        }
+
+    peers = [(s, d) for s in range(groups) for d in (0, 1, -1) if s or d]
+    barrier = pltpu.get_barrier_semaphore()
+    for s, d in peers:
+        pl.semaphore_signal(
+            barrier, inc=1, device_id=device(s, d), device_id_type=pl.DeviceIdType.MESH
+        )
+    times = position * steps + lax.broadcasted_iota(jnp.int32, (steps, BLK), 0)
+    weight = jnp.exp(times.astype(jnp.float32) * math.log(damping))
+    weight = jnp.where(times % 2 == 0, weight, -weight)
+    for b in range(blocks):
+        lanes = slice(b * BLK, (b + 1) * BLK)
+        own = traces_ref[:, lanes]
+        ext_ref[b + 1, TAPS:geo, :] = own
+        ext_ref[b + 1, geo : geo + 3, :] = xyz_ref[:, lanes]
+        ext_ref[b + 1, geo + 3 : geo + GEO, :] = jnp.zeros((GEO - 3, BLK), jnp.float32)
+        parts[b] = jnp.sum((weight * own).reshape(steps // 8, 8, BLK), axis=0)
+    pl.semaphore_wait(barrier, len(peers))
+    inner = pl.ds(TAPS, steps + GEO)
+    tail = pl.ds(steps, TAPS)
+    head = pl.ds(0, TAPS)
+    middle = pl.ds(1, blocks)
+    moves = [
+        (0, 1, ext_ref.at[blocks, inner], ext_ref.at[0, inner]),
+        (0, -1, ext_ref.at[1, inner], ext_ref.at[blocks + 1, inner]),
+        (1, 0, ext_ref.at[middle, tail], ext_ref.at[middle, head]),
+        (1, 1, ext_ref.at[blocks, tail], ext_ref.at[0, head]),
+        (1, -1, ext_ref.at[1, tail], ext_ref.at[blocks + 1, head]),
+    ]
+    for s, d in peers:
+        if d == 0:
+            moves.append((s, d, parts, slots.at[s, middle]))
+        elif d == 1:
+            moves.append((s, d, parts.at[blocks - 1], slots.at[s, 0]))
+        else:
+            moves.append((s, d, parts.at[0], slots.at[s, blocks + 1]))
+    copies = []
+    for i, (s, d, source, target) in enumerate(moves):
+        copy = pltpu.make_async_remote_copy(
+            src_ref=source,
+            dst_ref=target,
+            send_sem=send.at[i],
+            recv_sem=recv.at[i],
+            device_id=device(s, d),
+            device_id_type=pl.DeviceIdType.MESH,
+        )
+        copy.start()
+        copies.append(copy)
+    for copy in copies:
+        copy.wait()
+    around = jnp.where(position == 0, math.exp(NT * math.log(damping)), 1.0)
+    for c in range(blocks + 2):
+        ext_ref[c, :TAPS, :] = ext_ref[c, :TAPS, :] * around
+        total = parts[c - 1] if 1 <= c <= blocks else slots[0, c]
+        for s in range(1, groups):
+            total = total + slots[s, c]
+        nyquist_ref[c] = total
+
+
 def per_device(traces, centroids, near_list, pair_count):
     steps, width = traces.shape
     blocks = width // BLK
     groups = lax.axis_size("freq")
-    shards = lax.axis_size("panel")
     position = lax.axis_index("freq")
-    halo = lax.ppermute(
-        traces[steps - TAPS :], "freq", [(i, (i + 1) % groups) for i in range(groups)]
-    )
-    halo = halo * jnp.where(position == 0, math.exp(NT * math.log(damping)), 1.0)
-    times = position * steps + jnp.arange(steps, dtype=jnp.int32)
-    weight = jnp.exp(times.astype(jnp.float32) * math.log(damping))
-    weight = jnp.where(times % 2 == 0, weight, -weight)
-    nyquist = lax.psum(jnp.sum(weight[:, None] * traces, axis=0, keepdims=True), "freq")
-    pad = jnp.zeros((GEO - 4, width), jnp.float32)
-    own = jnp.concatenate([halo, traces, centroids, nyquist, pad], axis=0)
-    up = [(i, (i + 1) % shards) for i in range(shards)]
-    before = lax.ppermute(own[:, width - BLK :], "panel", up)
-    after = lax.ppermute(own[:, :BLK], "panel", [(j, i) for i, j in up])
-    pieces = [before] + [own[:, r * BLK : (r + 1) * BLK] for r in range(blocks)] + [after]
-    ext = jnp.stack(pieces, axis=0)
+    count = 5 + 3 * groups - 1
+    vmem = pl.BlockSpec(memory_space=pltpu.VMEM)
     smem = pl.BlockSpec(memory_space=pltpu.SMEM)
+    ext, nyquist = pl.pallas_call(
+        exchange,
+        out_shape=(
+            jax.ShapeDtypeStruct((blocks + 2, TAPS + steps + GEO, BLK), jnp.float32),
+            jax.ShapeDtypeStruct((blocks + 2, 8, BLK), jnp.float32),
+        ),
+        in_specs=[vmem, vmem],
+        out_specs=(vmem, vmem),
+        scratch_shapes=[
+            pltpu.VMEM((blocks, 8, BLK), jnp.float32),
+            pltpu.VMEM((groups, blocks + 2, 8, BLK), jnp.float32),
+            pltpu.SemaphoreType.DMA((count,)),
+            pltpu.SemaphoreType.DMA((count,)),
+        ],
+        compiler_params=pltpu.CompilerParams(collective_id=0, has_side_effects=True),
+    )(traces, centroids)
     return pl.pallas_call(
         near_field,
         out_shape=jax.ShapeDtypeStruct((steps, width), jnp.float32),
-        in_specs=[smem, smem, smem, pl.BlockSpec(memory_space=pltpu.VMEM)],
-        out_specs=pl.BlockSpec(memory_space=pltpu.VMEM),
+        in_specs=[smem, smem, smem, vmem, vmem],
+        out_specs=vmem,
         scratch_shapes=[
             pltpu.VMEM((blocks + 2, 2, steps + HALF, HALF * BLK), jnp.bfloat16),
             pltpu.VMEM((TAPS * BLK, 2 * BLK), jnp.bfloat16),
@@ -113,7 +192,7 @@
             pltpu.VMEM((blocks, 8, BLK), jnp.float32),
         ],
         compiler_params=pltpu.CompilerParams(vmem_limit_bytes=40 * 1024 * 1024),
-    )(near_list[0], pair_count, position.reshape(1).astype(jnp.int32), ext)
+    )(near_list[0], pair_count, position.reshape(1).astype(jnp.int32), ext, nyquist)
 
 
 def solution(mesh):

time: 40.6 us -> 34 us (0.84)
  the two profiles are of different devices: /device:TPU:0 before, /device:TPU:7 now
where the time goes in v2:
time: 34 us; the launch traced here: 33.4 us
  Pallas kernels  30.1 us (89%)
  local copies, waits for them, and re-layouts  2.6 us (8%)
  between operations  0.68 us (2%)
    pallas_call x1, Pallas kernels, per_device(): pl.pallas_call(near_field, out_shape=jax.ShapeDtypeStruct((steps, width),...  18 us
    pallas_call x1, Pallas kernels, per_device(): pl.pallas_call(exchange, out_shape=(jax.ShapeDtypeStruct((blocks + 2, TAP...  12.1 us
    unnamed x6, local copies, waits for them, and re-layouts  2.52 us

profile of v2, /device:TPU:7, one launch (start us, length us, event | category | flops | bytes accessed | tf_op | source)
XLA Modules:
  0.0 33.4 jit_solution(15478986869760167890)
XLA Ops:
  0.7 0.0 copy-start.2
  0.7 0.7 %copy-done.2 = s32[1,8,2]{1,2,0:T(2,128)S(1)} copy-done((s32[1,8,2]{1,2,0:T(2,128)S(1)}, s32[1,8,2]{1,2,0:T(2,128)}, u32[]{:S(2)}) %copy-start.2) | copy-done | bytes 88
  1.3 0.1 copy.5.list_ref
  1.4 12.1 %shard_map.46 = (f32[5,296,128]{2,1,0:T(8,128)}, f32[5,8,128]{2,1,0:T(8,128)}) custom-call(f32[256,384]{1,0:T(8,128)} %traces_ref.1, f32[3,384]{1,0:T(4,128)} %xyz_ref.1), custom_call_target="tpu_custom_call" | custom-call | tf_op jit(solution)/shard_map/pallas_call | solution.py:166
  13.5 0.0 copy-start
  13.5 1.1 %copy-done = f32[5,296,128]{2,1,0:T(8,128)S(1)} copy-done((f32[5,296,128]{2,1,0:T(8,128)S(1)}, f32[5,296,128]{2,1,0:T(8,128)}, u32[]{:S(2)}) %copy-start) | copy-done | bytes 757784
  14.7 0.0 copy-start.1
  14.7 0.7 %copy-done.1 = f32[5,8,128]{2,1,0:T(8,128)S(1)} copy-done((f32[5,8,128]{2,1,0:T(8,128)S(1)}, f32[5,8,128]{2,1,0:T(8,128)}, u32[]{:S(2)}) %copy-start.1) | copy-done | bytes 20504
  15.4 18.0 %shard_map.47 = f32[256,384]{1,0:T(8,128)} custom-call(s32[8,2]{1,0:T(8,128)S(1)} %copy.5.list_ref, s32[1]{0:T(128)S(6)} %copy.6.count_ref, s32[1]{0:T(128)} %bitcast.1.slab_ref, f32[5,296,128]{2,1,0:T(8,128)S(1)} %copy-done, f32[5,8,128]{2,1,0:T(8,128)S(1)} %copy-done.1), custom_call_target="tpu_custom_call" | custom-call | tf_op jit(solution)/shard_map/pallas_call | solution.py:182
Async XLA Ops:
  0.7 0.7 %copy-start.2 = (s32[1,8,2]{1,2,0:T(2,128)S(1)}, s32[1,8,2]{1,2,0:T(2,128)}, u32[]{:S(2)}) copy-start(s32[1,8,2]{1,2,0:T(2,128)} %param.6) | copy-start | bytes 196
  13.5 1.1 %copy-start = (f32[5,296,128]{2,1,0:T(8,128)S(1)}, f32[5,296,128]{2,1,0:T(8,128)}, u32[]{:S(2)}) copy-start(f32[5,296,128]{2,1,0:T(8,128)} %get-tuple-element.7.ext_ref) | copy-start | bytes 2273284
  14.7 0.7 %copy-start.1 = (f32[5,8,128]{2,1,0:T(8,128)S(1)}, f32[5,8,128]{2,1,0:T(8,128)}, u32[]{:S(2)}) copy-start(f32[5,8,128]{2,1,0:T(8,128)} %get-tuple-element.8.nyquist_ref) | copy-start | bytes 61444

commit v3 on v2

v3 whole, which is shorter than its diff:
```python
import math

import jax
import jax.numpy as jnp
from jax import lax
from jax.experimental import pallas as pl
from jax.experimental.pallas import tpu as pltpu
from jax.sharding import PartitionSpec as P

NT = 1024
BLK = 128
TAPS = 32
HALF = TAPS // 2
GEO = 8

damping = 0.999
time_step = 0.5
core_square = 0.01


def split(v):
    hi = v.astype(jnp.bfloat16)
    return hi, (v - hi.astype(jnp.float32)).astype(jnp.bfloat16)


def shift(shifted, ext, c, first, rows):
    for n in range(HALF):
        hi, lo = split(ext[c, first + HALF - n : first + HALF - n + rows, :])
        shifted[c, 0, first : first + rows, n * BLK : (n + 1) * BLK] = hi
        shifted[c, 1, first : first + rows, n * BLK : (n + 1) * BLK] = lo


def turn(geometry):
    return jnp.concatenate([geometry] * (BLK // GEO), axis=0).T


def contract(shifted, coeffs, col, steps):
    total = None
    for part in range(2):
        both = jnp.dot(
            shifted[col, part, HALF:, : HALF * BLK],
            coeffs[: HALF * BLK, :],
            preferred_element_type=jnp.float32,
        ) + jnp.dot(
            shifted[col, part, :steps, :],
            coeffs[HALF * BLK :, :],
            preferred_element_type=jnp.float32,
        )
        both = both[:, :BLK] + both[:, BLK:]
        total = both if total is None else total + both
    return total


def fill(coeffs, theirs, mine):
    square = jnp.full((BLK, BLK), core_square, jnp.float32)
    for a in range(3):
        diff = theirs[:, a : a + 1] - mine[a : a + 1, :]
        square = square + diff * diff
    dist = jnp.sqrt(square)
    x = dist * (1.0 / time_step)
    term = jnp.exp(-x) / (4.0 * math.pi * dist)

    def put(n, value):
        hi, lo = split(value)
        coeffs[n * BLK : (n + 1) * BLK, :BLK] = hi
        coeffs[n * BLK : (n + 1) * BLK, BLK:] = lo

    put(TAPS, term * jnp.exp(-damping * x))
    for n in range(TAPS):
        put(n, term)
        term = term * (x * (1.0 / (n + 1)))


def operator(
    list_ref,
    count_ref,
    traces_ref,
    xyz_ref,
    out_ref,
    ext_ref,
    shifted,
    even,
    odd,
    turned,
    acc,
    parts,
    slots,
    send,
    recv,
):
    steps, width = traces_ref.shape
    blocks = width // BLK
    geo = TAPS + steps
    groups = lax.axis_size("freq")
    shards = lax.axis_size("panel")
    position = lax.axis_index("freq")
    shard = lax.axis_index("panel")

    def device(ahead, side):
        return {
            "freq": lax.rem(position + ahead, groups),
            "panel": lax.rem(shard + side + shards, shards),
        }

    peers = [(s, d) for s in range(groups) for d in (0, 1, -1) if s or d]
    barrier = pltpu.get_barrier_semaphore()
    for s, d in peers:
        pl.semaphore_signal(
            barrier, inc=1, device_id=device(s, d), device_id_type=pl.DeviceIdType.MESH
        )
    times = position * steps + lax.broadcasted_iota(jnp.int32, (steps, BLK), 0)
    weight = jnp.exp(times.astype(jnp.float32) * math.log(damping))
    weight = jnp.where(times % 2 == 0, weight, -weight)
    for b in range(blocks):
        lanes = slice(b * BLK, (b + 1) * BLK)
        own = traces_ref[:, lanes]
        ext_ref[b + 1, TAPS:geo, :] = own
        ext_ref[b + 1, geo : geo + 3, :] = xyz_ref[:, lanes]
        ext_ref[b + 1, geo + 3 : geo + GEO, :] = jnp.zeros((GEO - 3, BLK), jnp.float32)
        parts[b] = jnp.sum((weight * own).reshape(steps // 8, 8, BLK), axis=0)
    pl.semaphore_wait(barrier, len(peers))
    inner = pl.ds(TAPS, steps + GEO)
    tail = pl.ds(steps, TAPS)
    head = pl.ds(0, TAPS)
    middle = pl.ds(1, blocks)
    moves = [
        (0, 1, ext_ref.at[blocks, inner], ext_ref.at[0, inner]),
        (0, -1, ext_ref.at[1, inner], ext_ref.at[blocks + 1, inner]),
        (1, 0, ext_ref.at[middle, tail], ext_ref.at[middle, head]),
        (1, 1, ext_ref.at[blocks, tail], ext_ref.at[0, head]),
        (1, -1, ext_ref.at[1, tail], ext_ref.at[blocks + 1, head]),
    ]
    for s, d in peers:
        if d == 0:
            moves.append((s, d, parts, slots.at[s, middle]))
        elif d == 1:
            moves.append((s, d, parts.at[blocks - 1], slots.at[s, 0]))
        else:
            moves.append((s, d, parts.at[0], slots.at[s, blocks + 1]))
    copies = []
    for i, (s, d, source, target) in enumerate(moves):
        copy = pltpu.make_async_remote_copy(
            src_ref=source,
            dst_ref=target,
            send_sem=send.at[i],
            recv_sem=recv.at[i],
            device_id=device(s, d),
            device_id_type=pl.DeviceIdType.MESH,
        )
        copy.start()
        copies.append(copy)
    for c in range(1, blocks + 1):
        turned[c] = turn(ext_ref[c, geo : geo + GEO, :])
    fill(even, turned[1], ext_ref[1, geo : geo + GEO, :])
    for c in range(1, blocks + 1):
        shift(shifted, ext_ref, c, TAPS, steps + HALF - TAPS)
    acc[...] = jnp.zeros_like(acc)
    local = lax.broadcasted_iota(jnp.int32, (steps, BLK), 0)
    growth = jnp.exp((position * steps + local).astype(jnp.float32) * -math.log(damping)) / NT
    growth = jnp.where(local % 2 == 0, -growth, growth)
    for copy in copies:
        copy.wait()
    around = jnp.where(position == 0, math.exp(NT * math.log(damping)), 1.0)
    for c in range(blocks + 2):
        ext_ref[c, :TAPS, :] = ext_ref[c, :TAPS, :] * around
        total = parts[c - 1] if 1 <= c <= blocks else slots[0, c]
        for s in range(1, groups):
            total = total + slots[s, c]
        hi, lo = split(growth * jnp.sum(total, axis=0, keepdims=True))
        shifted[c, 0, :steps, HALF * BLK :] = hi
        shifted[c, 1, :steps, HALF * BLK :] = lo
        if 1 <= c <= blocks:
            shift(shifted, ext_ref, c, 0, TAPS)
        else:
            shift(shifted, ext_ref, c, 0, steps + HALF)
            turned[c] = turn(ext_ref[c, geo : geo + GEO, :])
    pairs = list_ref.shape[0]

    def step(slot, now, later):
        following = jnp.minimum(slot + 1, pairs - 1)
        row = list_ref[following, 0]
        col = list_ref[following, 1]
        mine = ext_ref[row + 1, geo : geo + GEO, :]
        theirs = turned[col]
        total = contract(shifted, now, list_ref[slot, 1], steps)
        fill(later, theirs, mine)
        target = jnp.where(slot < count_ref[0], list_ref[slot, 0], blocks)
        for r in range(blocks):
            acc[r] = acc[r] + jnp.where(target == r, total, 0.0)

    def two(i, carry):
        step(2 * i, even, odd)
        step(2 * i + 1, odd, even)
        return carry

    lax.fori_loop(0, pairs // 2, two, 0)
    for r in range(blocks):
        out_ref[:, r * BLK : (r + 1) * BLK] = acc[r]


def per_device(traces, centroids, near_list, pair_count):
    steps, width = traces.shape
    blocks = width // BLK
    groups = lax.axis_size("freq")
    count = 5 + 3 * groups - 1
    depth = (TAPS + 1) * BLK
    vmem = pl.BlockSpec(memory_space=pltpu.VMEM)
    smem = pl.BlockSpec(memory_space=pltpu.SMEM)
    return pl.pallas_call(
        operator,
        out_shape=jax.ShapeDtypeStruct((steps, width), jnp.float32),
        in_specs=[smem, smem, vmem, vmem],
        out_specs=vmem,
        scratch_shapes=[
            pltpu.VMEM((blocks + 2, TAPS + steps + GEO, BLK), jnp.float32),
            pltpu.VMEM((blocks + 2, 2, steps + HALF, (HALF + 1) * BLK), jnp.bfloat16),
            pltpu.VMEM((depth, 2 * BLK), jnp.bfloat16),
            pltpu.VMEM((depth, 2 * BLK), jnp.bfloat16),
            pltpu.VMEM((blocks + 2, BLK, BLK), jnp.float32),
            pltpu.VMEM((blocks, steps, BLK), jnp.float32),
            pltpu.VMEM((blocks, 8, BLK), jnp.float32),
            pltpu.VMEM((groups, blocks + 2, 8, BLK), jnp.float32),
            pltpu.SemaphoreType.DMA((count,)),
            pltpu.SemaphoreType.DMA((count,)),
        ],
        compiler_params=pltpu.CompilerParams(
            collective_id=0, has_side_effects=True, vmem_limit_bytes=40 * 1024 * 1024
        ),
    )(near_list[0], pair_count, traces, centroids)


def solution(mesh):
    in_specs = (
        P("freq", ("grp", "panel")),
        P(None, ("grp", "panel")),
        P(("grp", "panel"), None, None),
        P(("grp", "panel")),
    )
    out_specs = P("freq", ("grp", "panel"))
    return jax.shard_map(
        per_device, mesh=mesh, in_specs=in_specs, out_specs=out_specs, check_vma=False
    )
```

time: 34 us -> 28.1 us (0.83)
  the two profiles are of different devices: /device:TPU:7 before, /device:TPU:0 now
where the time goes in v3:
time: 28.1 us; the launch traced here: 27.9 us
  Pallas kernels  24.7 us (88%)
  local copies, waits for them, and re-layouts  2.5 us (9%)
  between operations  0.68 us (2%)
    pallas_call x1, Pallas kernels, per_device(): pl.pallas_call(operator, out_shape=jax.ShapeDtypeStruct((steps, width), j...  24.7 us
    unnamed x5, local copies, waits for them, and re-layouts  1.75 us
    squeeze x1, local copies, waits for them, and re-layouts, per_device(): near_list[0]  0.75 us

profile of v3, /device:TPU:0, one launch (start us, length us, event | category | flops | bytes accessed | tf_op | source)
XLA Modules:
  0.0 27.9 jit_solution(3869741633509356125)
XLA Ops:
  0.0 0.0 copy-start.1
  0.7 0.8 %copy.5.list_ref = s32[8,2]{1,0:T(8,128)S(1)} copy(s32[8,2]{0,1:T(2,128)} %bitcast.1) | data formatting | bytes 128 | tf_op jit(solution)/shard_map/squeeze | solution.py:229
  1.4 0.0 copy-done.1
  1.4 0.0 copy-start
  1.4 1.0 %copy-done = f32[256,384]{1,0:T(8,128)S(1)} copy-done((f32[256,384]{1,0:T(8,128)S(1)}, f32[256,384]{1,0:T(8,128)}, u32[]{:S(2)}) %copy-start) | copy-done | bytes 393240
  2.4 24.7 %shard_map.46 = f32[256,384]{1,0:T(8,128)S(1)} custom-call(s32[8,2]{1,0:T(8,128)S(1)} %copy.5.list_ref, s32[1]{0:T(128)S(6)} %copy.7.count_ref, f32[256,384]{1,0:T(8,128)S(1)} %copy-done, f32[3,384]{1,0:T(4,128)S(1)} %copy-done.1), custom_call_target="tpu_custom_call" | custom-call | tf_op jit(solution)/shard_map/pallas_call | solution.py:209
  27.1 0.7 %copy.8 = f32[256,384]{1,0:T(8,128)} copy(f32[256,384]{1,0:T(8,128)S(1)} %shard_map.46) | data formatting | bytes 786432
Async XLA Ops:
  0.0 1.4 %copy-start.1 = (f32[3,384]{1,0:T(4,128)S(1)}, f32[3,384]{1,0:T(4,128)}, u32[]{:S(2)}) copy-start(f32[3,384]{1,0:T(4,128)} %xyz_ref.1) | copy-start | bytes 13828
  1.4 1.0 %copy-start = (f32[256,384]{1,0:T(8,128)S(1)}, f32[256,384]{1,0:T(8,128)}, u32[]{:S(2)}) copy-start(f32[256,384]{1,0:T(8,128)} %traces_ref.1) | copy-start | bytes 1179652

commit v4 on v3

v4 whole, which is shorter than its diff:
```python
import math

import jax
import jax.numpy as jnp
from jax import lax
from jax.experimental import pallas as pl
from jax.experimental.pallas import tpu as pltpu
from jax.sharding import PartitionSpec as P

NT = 1024
BLK = 128
TAPS = 32
HALF = TAPS // 2
PAIR = HALF // 2
GEO = 8

damping = 0.999
time_step = 0.5
core_square = 0.01


def split(v):
    hi = v.astype(jnp.bfloat16)
    return hi, (v - hi.astype(jnp.float32)).astype(jnp.bfloat16)


def shift(high, low, ext, c, first, rows):
    for n in range(HALF):
        hi, lo = split(ext[c, first + HALF - n : first + HALF - n + rows, :])
        high[c, first : first + rows, n * BLK : (n + 1) * BLK] = hi
        if n < PAIR:
            low[c, first : first + rows, n * BLK : (n + 1) * BLK] = lo


def turn(geometry):
    return jnp.concatenate([geometry] * (BLK // GEO), axis=0).T


def product(x, y):
    return jnp.dot(x, y, preferred_element_type=jnp.float32)


def contract(high, low, coeffs, col, steps):
    rows = steps + HALF
    one, two, three = HALF * BLK, (HALF + PAIR) * BLK, (HALF + 2 * PAIR) * BLK
    both = product(high[col, HALF:, :], coeffs[:one, :])
    total = both[:, :BLK] + both[:, BLK:]
    cross = product(low[col], coeffs[one:two, :])
    total = total + (cross[HALF:rows, :BLK] + cross[HALF - PAIR : rows - PAIR, BLK:])
    far = product(high[col, :, PAIR * BLK :], coeffs[two:three, :])
    return total + (far[PAIR : PAIR + steps, :BLK] + far[:steps, BLK:])


def fill(coeffs, sample, theirs, mine):
    square = jnp.full((BLK, BLK), core_square, jnp.float32)
    for a in range(3):
        diff = theirs[:, a : a + 1] - mine[a : a + 1, :]
        square = square + diff * diff
    dist = jnp.sqrt(square)
    x = dist * (1.0 / time_step)
    term = jnp.exp(-x) / (4.0 * math.pi * dist)
    sample[...] = term * jnp.exp(-damping * x)

    def put(place, half, value):
        coeffs[place * BLK : (place + 1) * BLK, half * BLK : (half + 1) * BLK] = value

    for n in range(TAPS):
        if n < HALF:
            hi, lo = split(term)
            put(n, 0, hi)
            put(n, 1, lo)
        else:
            hi = term.astype(jnp.bfloat16)
        put(HALF + n // HALF * PAIR + n % PAIR, n // PAIR % 2, hi)
        term = term * (x * (1.0 / (n + 1)))


def operator(
    list_ref,
    count_ref,
    traces_ref,
    xyz_ref,
    out_ref,
    ext_ref,
    high,
    low,
    even,
    odd,
    even_sample,
    odd_sample,
    turned,
    acc,
    last,
    parts,
    slots,
    send,
    recv,
    load,
):
    steps, width = traces_ref.shape
    blocks = width // BLK
    geo = TAPS + steps
    groups = lax.axis_size("freq")
    shards = lax.axis_size("panel")
    position = lax.axis_index("freq")
    shard = lax.axis_index("panel")

    def device(ahead, side):
        return {
            "freq": lax.rem(position + ahead, groups),
            "panel": lax.rem(shard + side + shards, shards),
        }

    peers = [(s, d) for s in range(groups) for d in (0, 1, -1) if s or d]
    barrier = pltpu.get_barrier_semaphore()
    for s, d in peers:
        pl.semaphore_signal(
            barrier, inc=1, device_id=device(s, d), device_id_type=pl.DeviceIdType.MESH
        )
    loads = [
        pltpu.make_async_copy(
            traces_ref.at[:, pl.ds(b * BLK, BLK)],
            ext_ref.at[b + 1, pl.ds(TAPS, steps)],
            load.at[b],
        )
        for b in range(blocks)
    ]
    for copy in loads:
        copy.start()
    times = position * steps + lax.broadcasted_iota(jnp.int32, (steps, BLK), 0)
    weight = jnp.exp(times.astype(jnp.float32) * math.log(damping))
    weight = jnp.where(times % 2 == 0, weight, -weight)
    for b in range(blocks):
        lanes = slice(b * BLK, (b + 1) * BLK)
        ext_ref[b + 1, geo : geo + 3, :] = xyz_ref[:, lanes]
        ext_ref[b + 1, geo + 3 : geo + GEO, :] = jnp.zeros((GEO - 3, BLK), jnp.float32)
    for b in range(blocks):
        loads[b].wait()
        own = ext_ref[b + 1, TAPS:geo, :]
        parts[b] = jnp.sum((weight * own).reshape(steps // 8, 8, BLK), axis=0)
    pl.semaphore_wait(barrier, len(peers))
    inner = pl.ds(TAPS, steps + GEO)
    tail = pl.ds(steps, TAPS)
    head = pl.ds(0, TAPS)
    middle = pl.ds(1, blocks)
    moves = [
        (0, 1, ext_ref.at[blocks, inner], ext_ref.at[0, inner]),
        (0, -1, ext_ref.at[1, inner], ext_ref.at[blocks + 1, inner]),
        (1, 0, ext_ref.at[middle, tail], ext_ref.at[middle, head]),
        (1, 1, ext_ref.at[blocks, tail], ext_ref.at[0, head]),
        (1, -1, ext_ref.at[1, tail], ext_ref.at[blocks + 1, head]),
    ]
    for s, d in peers:
        if d == 0:
            moves.append((s, d, parts, slots.at[s, middle]))
        elif d == 1:
            moves.append((s, d, parts.at[blocks - 1], slots.at[s, 0]))
        else:
            moves.append((s, d, parts.at[0], slots.at[s, blocks + 1]))
    copies = []
    for i, (s, d, source, target) in enumerate(moves):
        copy = pltpu.make_async_remote_copy(
            src_ref=source,
            dst_ref=target,
            send_sem=send.at[i],
            recv_sem=recv.at[i],
            device_id=device(s, d),
            device_id_type=pl.DeviceIdType.MESH,
        )
        copy.start()
        copies.append(copy)
    for c in range(1, blocks + 1):
        turned[c] = turn(ext_ref[c, geo : geo + GEO, :])
    fill(even, even_sample, turned[1], ext_ref[1, geo : geo + GEO, :])
    for c in range(1, blocks + 1):
        shift(high, low, ext_ref, c, TAPS, steps + HALF - TAPS)
    acc[...] = jnp.zeros_like(acc)
    last[...] = jnp.zeros_like(last)
    local = lax.broadcasted_iota(jnp.int32, (steps, BLK), 0)
    growth = jnp.exp((position * steps + local).astype(jnp.float32) * -math.log(damping)) / NT
    growth = jnp.where(local % 2 == 0, -growth, growth)
    for copy in copies:
        copy.wait()
    around = jnp.where(position == 0, math.exp(NT * math.log(damping)), 1.0)
    for c in range(blocks + 2):
        ext_ref[c, :TAPS, :] = ext_ref[c, :TAPS, :] * around
        total = parts[c - 1] if 1 <= c <= blocks else slots[0, c]
        for s in range(1, groups):
            total = total + slots[s, c]
        place = lax.broadcasted_iota(jnp.int32, (GEO, BLK), 0)
        total = jnp.sum(total, axis=0, keepdims=True)
        turned[c] = turn(jnp.where(place == 3, total, ext_ref[c, geo : geo + GEO, :]))
        if 1 <= c <= blocks:
            shift(high, low, ext_ref, c, 0, TAPS)
        else:
            shift(high, low, ext_ref, c, 0, steps + HALF)
    pairs = list_ref.shape[1]

    def step(slot, now, now_sample, later, later_sample):
        following = jnp.minimum(slot + 1, pairs - 1)
        row = list_ref[0, following]
        col = list_ref[1, following]
        mine = ext_ref[row + 1, geo : geo + GEO, :]
        theirs = turned[col]
        col = list_ref[1, slot]
        total = contract(high, low, now, col, steps)
        sums = jnp.sum(now_sample[...] * turned[col][:, 3:4], axis=0, keepdims=True)
        fill(later, later_sample, theirs, mine)
        target = jnp.where(slot < count_ref[0], list_ref[0, slot], blocks)
        for r in range(blocks):
            acc[r] = acc[r] + jnp.where(target == r, total, 0.0)
            last[r] = last[r] + jnp.where(target == r, sums, 0.0)

    def two(i, carry):
        step(2 * i, even, even_sample, odd, odd_sample)
        step(2 * i + 1, odd, odd_sample, even, even_sample)
        return carry

    lax.fori_loop(0, pairs // 2, two, 0)
    for r in range(blocks):
        out_ref[:, r * BLK : (r + 1) * BLK] = acc[r] + growth * last[r, 0:1, :]


def per_device(traces, centroids, near_list, pair_count):
    steps, width = traces.shape
    blocks = width // BLK
    groups = lax.axis_size("freq")
    count = 5 + 3 * groups - 1
    depth = (HALF + 2 * PAIR) * BLK
    vmem = pl.BlockSpec(memory_space=pltpu.VMEM)
    smem = pl.BlockSpec(memory_space=pltpu.SMEM)
    return pl.pallas_call(
        operator,
        out_shape=jax.ShapeDtypeStruct((steps, width), jnp.float32),
        in_specs=[smem, smem, pl.BlockSpec(memory_space=pltpu.HBM), vmem],
        out_specs=vmem,
        scratch_shapes=[
            pltpu.VMEM((blocks + 2, TAPS + steps + GEO, BLK), jnp.float32),
            pltpu.VMEM((blocks + 2, steps + HALF, HALF * BLK), jnp.bfloat16),
            pltpu.VMEM((blocks + 2, steps + HALF, PAIR * BLK), jnp.bfloat16),
            pltpu.VMEM((depth, 2 * BLK), jnp.bfloat16),
            pltpu.VMEM((depth, 2 * BLK), jnp.bfloat16),
            pltpu.VMEM((BLK, BLK), jnp.float32),
            pltpu.VMEM((BLK, BLK), jnp.float32),
            pltpu.VMEM((blocks + 2, BLK, BLK), jnp.float32),
            pltpu.VMEM((blocks, steps, BLK), jnp.float32),
            pltpu.VMEM((blocks, 8, BLK), jnp.float32),
            pltpu.VMEM((blocks, 8, BLK), jnp.float32),
            pltpu.VMEM((groups, blocks + 2, 8, BLK), jnp.float32),
            pltpu.SemaphoreType.DMA((count,)),
            pltpu.SemaphoreType.DMA((count,)),
            pltpu.SemaphoreType.DMA((blocks,)),
        ],
        compiler_params=pltpu.CompilerParams(
            collective_id=0, has_side_effects=True, vmem_limit_bytes=60 * 1024 * 1024
        ),
    )(near_list[0].T, pair_count, traces, centroids)


def solution(mesh):
    in_specs = (
        P("freq", ("grp", "panel")),
        P(None, ("grp", "panel")),
        P(("grp", "panel"), None, None),
        P(("grp", "panel")),
    )
    out_specs = P("freq", ("grp", "panel"))
    return jax.shard_map(
        per_device, mesh=mesh, in_specs=in_specs, out_specs=out_specs, check_vma=False
    )
```

time: 28.1 us -> 24.2 us (0.86)
  Pallas kernels: 24.7 us -> 21.6 us
  local copies, waits for them, and re-layouts: 2.5 us -> 1.77 us
    pallas_call x1, Pallas kernels: 24.7 us -> 21.6 us  [per_device(): pl.pallas_call(operator, out_shape=jax.ShapeDtypeStruct((steps, width), j...]
    squeeze x1 -> x0, local copies, waits for them, and re-layouts: 0.75 us -> none  [per_device(): near_list[0]]
    unnamed x5 -> x1, local copies, waits for them, and re-layouts: 1.75 us -> 1.77 us
where the time goes in v4:
time: 24.2 us; the launch traced here: 24 us
  Pallas kernels  21.6 us (89%)
  local copies, waits for them, and re-layouts  1.77 us (7%)
  between operations  0.66 us (3%)
    pallas_call x1, Pallas kernels, per_device(): pl.pallas_call(operator, out_shape=jax.ShapeDtypeStruct((steps, width), j...  21.6 us
    unnamed x1, local copies, waits for them, and re-layouts  1.77 us

profile of v4, /device:TPU:0, one launch (start us, length us, event | category | flops | bytes accessed | tf_op | source)
XLA Modules:
  0.0 24.0 jit_solution(9845972987243870645)
XLA Ops:
  0.7 21.6 %shard_map.46 = f32[256,384]{1,0:T(8,128)} custom-call(s32[2,8]{1,0:T(2,128)} %bitcast.3, s32[1]{0:T(128)S(6)} %copy.6.count_ref, f32[256,384]{1,0:T(8,128)} %traces_ref.1, f32[3,384]{1,0:T(4,128)} %xyz_ref.1), custom_call_target="tpu_custom_call" | custom-call | tf_op jit(solution)/shard_map/pallas_call | solution.py:232
  22.2 1.8 %copy.7 = f32[256,384]{1,0:T(8,128)} copy(f32[256,384]{1,0:T(8,128)} %shard_map.46) | data formatting | bytes 786432

commit v5 on v4

--- a/solution.py
+++ b/solution.py
@@ -138,6 +138,8 @@
         loads[b].wait()
         own = ext_ref[b + 1, TAPS:geo, :]
         parts[b] = jnp.sum((weight * own).reshape(steps // 8, 8, BLK), axis=0)
+    turned[1] = turn(ext_ref[1, geo : geo + GEO, :])
+    fill(even, even_sample, turned[1], ext_ref[1, geo : geo + GEO, :])
     pl.semaphore_wait(barrier, len(peers))
     inner = pl.ds(TAPS, steps + GEO)
     tail = pl.ds(steps, TAPS)
@@ -170,16 +172,16 @@
         copy.start()
         copies.append(copy)
     for c in range(1, blocks + 1):
-        turned[c] = turn(ext_ref[c, geo : geo + GEO, :])
-    fill(even, even_sample, turned[1], ext_ref[1, geo : geo + GEO, :])
-    for c in range(1, blocks + 1):
         shift(high, low, ext_ref, c, TAPS, steps + HALF - TAPS)
     acc[...] = jnp.zeros_like(acc)
     last[...] = jnp.zeros_like(last)
     local = lax.broadcasted_iota(jnp.int32, (steps, BLK), 0)
     growth = jnp.exp((position * steps + local).astype(jnp.float32) * -math.log(damping)) / NT
     growth = jnp.where(local % 2 == 0, -growth, growth)
-    for copy in copies:
+    for copy, c in zip(copies[:2], (0, blocks + 1)):
+        copy.wait()
+        shift(high, low, ext_ref, c, TAPS, steps + HALF - TAPS)
+    for copy in copies[2:]:
         copy.wait()
     around = jnp.where(position == 0, math.exp(NT * math.log(damping)), 1.0)
     for c in range(blocks + 2):
@@ -190,10 +192,7 @@
         place = lax.broadcasted_iota(jnp.int32, (GEO, BLK), 0)
         total = jnp.sum(total, axis=0, keepdims=True)
         turned[c] = turn(jnp.where(place == 3, total, ext_ref[c, geo : geo + GEO, :]))
-        if 1 <= c <= blocks:
-            shift(high, low, ext_ref, c, 0, TAPS)
-        else:
-            shift(high, low, ext_ref, c, 0, steps + HALF)
+        shift(high, low, ext_ref, c, 0, TAPS)
     pairs = list_ref.shape[1]
 
     def step(slot, now, now_sample, later, later_sample):

time: 24.2 us -> 23.9 us (0.988)
  Pallas kernels: 21.6 us -> 21.2 us
    pallas_call x1, Pallas kernels: 21.6 us -> 21.2 us  [per_device(): pl.pallas_call(operator, out_shape=jax.ShapeDtypeStruct((steps, width), j...]
where the time goes in v5:
time: 23.9 us; the launch traced here: 23.6 us
  Pallas kernels  21.2 us (89%)
  local copies, waits for them, and re-layouts  1.77 us (7%)
  between operations  0.66 us (3%)
    pallas_call x1, Pallas kernels, per_device(): pl.pallas_call(operator, out_shape=jax.ShapeDtypeStruct((steps, width), j...  21.2 us
    unnamed x1, local copies, waits for them, and re-layouts  1.77 us

profile of v5, /device:TPU:0, one launch (start us, length us, event | category | flops | bytes accessed | tf_op | source)
XLA Modules:
  0.0 23.6 jit_solution(1447586495978670027)
XLA Ops:
  0.7 21.2 %shard_map.46 = f32[256,384]{1,0:T(8,128)} custom-call(s32[2,8]{1,0:T(2,128)} %bitcast.3, s32[1]{0:T(128)S(6)} %copy.6.count_ref, f32[256,384]{1,0:T(8,128)} %traces_ref.1, f32[3,384]{1,0:T(4,128)} %xyz_ref.1), custom_call_target="tpu_custom_call" | custom-call | tf_op jit(solution)/shard_map/pallas_call | solution.py:231
  21.9 1.8 %copy.7 = f32[256,384]{1,0:T(8,128)} copy(f32[256,384]{1,0:T(8,128)} %shard_map.46) | data formatting | bytes 786432

commit v6 on v5

--- a/solution.py
+++ b/solution.py
@@ -169,8 +169,9 @@
             device_id=device(s, d),
             device_id_type=pl.DeviceIdType.MESH,
         )
+        copies.append(copy)
+    for copy in copies[2:] + copies[:2]:
         copy.start()
-        copies.append(copy)
     for c in range(1, blocks + 1):
         shift(high, low, ext_ref, c, TAPS, steps + HALF - TAPS)
     acc[...] = jnp.zeros_like(acc)

time: 23.9 us -> 24 us (level)
  no operation moved by 1% of the time
where the time goes in v6:
time: 24 us; the launch traced here: 23.7 us
  Pallas kernels  21.3 us (89%)
  local copies, waits for them, and re-layouts  1.77 us (7%)
  between operations  0.66 us (3%)
    pallas_call x1, Pallas kernels, per_device(): pl.pallas_call(operator, out_shape=jax.ShapeDtypeStruct((steps, width), j...  21.3 us
    unnamed x1, local copies, waits for them, and re-layouts  1.77 us

profile of v6, /device:TPU:0, one launch (start us, length us, event | category | flops | bytes accessed | tf_op | source)
XLA Modules:
  0.0 23.7 jit_solution(16186377895976820607)
XLA Ops:
  0.7 21.3 %shard_map.46 = f32[256,384]{1,0:T(8,128)} custom-call(s32[2,8]{1,0:T(2,128)} %bitcast.3, s32[1]{0:T(128)S(6)} %copy.6.count_ref, f32[256,384]{1,0:T(8,128)} %traces_ref.1, f32[3,384]{1,0:T(4,128)} %xyz_ref.1), custom_call_target="tpu_custom_call" | custom-call | tf_op jit(solution)/shard_map/pallas_call | solution.py:232
  22.0 1.8 %copy.7 = f32[256,384]{1,0:T(8,128)} copy(f32[256,384]{1,0:T(8,128)} %shard_map.46) | data formatting | bytes 786432
